TPU v7x, 32 devices: a whole 2x2x4 slice. The times are simulated.
32 devices in a mesh: fsdp: 8 (over z, core), seq: 4 (over y, x).
Axes of the slice: x: 2, y: 2, z: 4, core: 2. Of those that a mesh axis runs over, the one named last changes fastest.
Arguments:
- hidden_in: bfloat16 [8192, 1536], P(('fsdp', 'seq')), may hold values from -12 to 12
- cotangent: bfloat16 [8192, 1536], P(('fsdp', 'seq')), may hold values from -6 to 6
- segment_ids: int32 [8, 1024], P('fsdp', 'seq'), may hold values from 0 to 3, never falling along the last dimension, each value on 1 to 512 neighbouring positions
- w_qkv: bfloat16 [1536, 3072], P('fsdp', 'seq'), may hold values from -1.5 to 1.5
- w_out: bfloat16 [1536, 1536], P('fsdp', 'seq'), may hold values from -0.625 to 0.625
- w_gate: bfloat16 [1536, 4096], P('fsdp', 'seq'), may hold values from -0.15625 to 0.15625
- w_up: bfloat16 [1536, 4096], P('fsdp', 'seq'), may hold values from -0.15625 to 0.15625
- w_down: bfloat16 [4096, 1536], P('fsdp', 'seq'), may hold values from -0.09375 to 0.09375
- gain_attn: bfloat16 [1536], P(('fsdp', 'seq')), may hold values from 0.099609375 to 1.8984375
- gain_mlp: bfloat16 [1536], P(('fsdp', 'seq')), may hold values from 0.099609375 to 1.8984375
Outputs:
- output: float32 [8192, 1536], P(('fsdp', 'seq'))
- d_input: float32 [8192, 1536], P(('fsdp', 'seq'))
- g_qkv: float32 [1536, 3072], P('fsdp', 'seq')
- g_out: float32 [1536, 1536], P('fsdp', 'seq')
- g_gate: float32 [1536, 4096], P('fsdp', 'seq')
- g_up: float32 [1536, 4096], P('fsdp', 'seq')
- g_down: float32 [4096, 1536], P('fsdp', 'seq')
- g_gain_attn: float32 [1536], P(('fsdp', 'seq'))
- g_gain_mlp: float32 [1536], P(('fsdp', 'seq'))
Inputs may be any that keep to these rules, and one draw needn't show every extreme that they name: `segment_ids`: document numbers never fall along a row; a document has 1 to 512 tokens.
All inputs are finite; a program needn't handle non-finite values.
Results may differ from a plain program's by a relative error of at most 0.02.
Values may be sent and summed in bfloat16 or wider, within the bound.
A program may use at most 320 MiB of HBM per device.

v0:
```python
import math
import jax
import jax.numpy as jnp
from jax import lax
from jax.sharding import PartitionSpec as P

HEAD_DIM = 96
EPSILON = 1e-05
ROPE_BASE = 100000.0
NEGATIVE = -1e30


def rope_tables(ids):
    length = ids.shape[0]
    first = jnp.sum((ids[None, :] < ids[:, None]).astype(jnp.int32), axis=1)
    positions = jnp.arange(length, dtype=jnp.int32) - first
    half_dim = HEAD_DIM // 2
    freq_steps = jnp.arange(half_dim, dtype=jnp.float32)
    inverse = jnp.exp(freq_steps * (-2.0 * math.log(ROPE_BASE) / HEAD_DIM))
    angles = positions.astype(jnp.float32)[:, None] * inverse[None, :]
    return (jnp.cos(angles), jnp.sin(angles))


def rotate(block, cosine_table, sine_table):
    half_dim = block.shape[-1] // 2
    lower, upper = (block[..., :half_dim], block[..., half_dim:])
    return jnp.concatenate(
        [lower * cosine_table - upper * sine_table, upper * cosine_table + lower * sine_table],
        axis=-1,
    )


def inv_rms(values):
    return lax.rsqrt(jnp.mean(values * values, axis=-1, keepdims=True) + EPSILON)


def norm_back(grad_in, values, row_scale, gain_vec):
    weighted = grad_in * gain_vec
    d_values = row_scale * (
        weighted
        - values * (row_scale * row_scale) * jnp.mean(weighted * values, axis=-1, keepdims=True)
    )
    return (d_values, jnp.sum(grad_in * values * row_scale, axis=0))


def contract_rows(left, right):
    return lax.dot_general(
        left, right, (((0,), (0,)), ((), ())), preferred_element_type=jnp.float32
    )


def times(left, right):
    return jnp.dot(left, right, preferred_element_type=jnp.float32)


def times_trans(left, right):
    return lax.dot_general(
        left, right, (((1,), (1,)), ((), ())), preferred_element_type=jnp.float32
    )


def attend_forward(group, allowed, score_scale):
    queries, keys, vals = (group[:, :2], group[:, 2], group[:, 3])
    scores = jnp.einsum("qhd,kd->hqk", queries, keys, preferred_element_type=jnp.float32)
    scores = jnp.where(allowed[None], scores * score_scale, NEGATIVE)
    row_max = jnp.max(scores, axis=-1, keepdims=True)
    lse = row_max + jnp.log(jnp.sum(jnp.exp(scores - row_max), axis=-1, keepdims=True))
    weights = jnp.where(allowed[None], jnp.exp(scores - lse), 0.0).astype(jnp.bfloat16)
    mixed = jnp.einsum("hqk,kd->qhd", weights, vals, preferred_element_type=jnp.float32)
    return (mixed.astype(jnp.bfloat16), lse)


def attend_backward(group, mixed, lse, d_mixed, allowed, score_scale):
    queries, keys, vals = (group[:, :2], group[:, 2], group[:, 3])
    delta = jnp.sum(d_mixed.astype(jnp.float32) * mixed.astype(jnp.float32), axis=-1)
    scores = jnp.einsum("qhd,kd->hqk", queries, keys, preferred_element_type=jnp.float32)
    probs = jnp.where(allowed[None], jnp.exp(scores * score_scale - lse), 0.0)
    d_vals = jnp.einsum(
        "hqk,qhd->kd", probs.astype(jnp.bfloat16), d_mixed, preferred_element_type=jnp.float32
    )
    d_probs = jnp.einsum("qhd,kd->hqk", d_mixed, vals, preferred_element_type=jnp.float32)
    d_scores = (probs * (d_probs - jnp.transpose(delta)[:, :, None])).astype(jnp.bfloat16)
    d_q = jnp.einsum("hqk,kd->qhd", d_scores, keys, preferred_element_type=jnp.float32)
    d_k = jnp.einsum("hqk,qhd->kd", d_scores, queries, preferred_element_type=jnp.float32)
    return (d_q * score_scale, d_k * score_scale, d_vals)


def body(
    hidden_in, cotangent, segment_ids, w_qkv, w_out, w_gate, w_up, w_down, gain_attn, gain_mlp
):
    rows = hidden_in.shape[0]
    fsdp = lax.axis_size("fsdp")
    seq = lax.axis_size("seq")
    ratio = fsdp // seq
    scale = 1.0 / math.sqrt(HEAD_DIM)
    length = rows * seq
    moves = [
        (f * seq + s, (f % ratio * seq + s) * seq + f // ratio)
        for f in range(fsdp)
        for s in range(seq)
    ]
    back = [(there, here) for here, there in moves]

    def gather_rows(shard):
        height, width = shard.shape
        moved = lax.ppermute(shard, ("fsdp", "seq"), moves)
        blocks = lax.all_gather(moved, "fsdp", axis=0, tiled=False)
        blocks = blocks.reshape(ratio, seq, height, width)
        return jnp.transpose(blocks, (0, 2, 1, 3)).reshape(ratio * height, seq * width)

    def scatter_rows(grad):
        height, width = (grad.shape[0] // ratio, grad.shape[1] // seq)
        blocks = grad.astype(jnp.bfloat16).reshape(ratio, height, seq, width)
        blocks = jnp.transpose(blocks, (0, 2, 1, 3)).reshape(fsdp, height, width)
        own = lax.psum_scatter(blocks, "fsdp", scatter_dimension=0, tiled=False)
        return lax.ppermute(own, ("fsdp", "seq"), back).astype(jnp.float32)

    def gather_cols(shard):
        return lax.all_gather(shard, "fsdp", axis=0, tiled=True)

    def scatter_cols(grad):
        return lax.psum_scatter(
            grad.astype(jnp.bfloat16), "fsdp", scatter_dimension=0, tiled=True
        ).astype(jnp.float32)

    def gather_tokens(block):
        return lax.all_gather(block, "seq", axis=0, tiled=True)

    def scatter_tokens(partial):
        return lax.psum_scatter(
            partial.astype(jnp.bfloat16), "seq", scatter_dimension=0, tiled=True
        ).astype(jnp.float32)

    gains = lax.all_gather(
        jnp.stack([gain_attn, gain_mlp]), ("fsdp", "seq"), axis=1, tiled=True
    ).astype(jnp.float32)
    gain_one, gain_two = (gains[0], gains[1])
    ids = lax.all_gather(segment_ids, "seq", axis=1, tiled=True)[0]
    hidden_all = gather_tokens(hidden_in)
    cot_all = gather_tokens(cotangent)
    cols_qkv = gather_cols(w_qkv)
    rows_out = gather_rows(w_out)
    cols_gate = gather_cols(w_gate)
    cols_up = gather_cols(w_up)
    rows_down = gather_rows(w_down)
    tok = jnp.arange(length, dtype=jnp.int32)
    allowed = (ids[:, None] == ids[None, :]) & (tok[None, :] <= tok[:, None])
    cosine, sine = rope_tables(ids)
    values_all = hidden_all.astype(jnp.float32)
    normed_one = (values_all * inv_rms(values_all) * gain_one).astype(jnp.bfloat16)
    groups = cols_qkv.shape[1] // (4 * HEAD_DIM)
    projected = times(normed_one, cols_qkv).reshape(length, groups, 4, HEAD_DIM)
    packed = jnp.concatenate(
        [
            rotate(projected[:, :, :3], cosine[:, None, None, :], sine[:, None, None, :]),
            projected[:, :, 3:],
        ],
        axis=2,
    ).astype(jnp.bfloat16)
    forward = [attend_forward(packed[:, g], allowed, scale) for g in range(groups)]
    attn = jnp.stack([mixed for mixed, _ in forward], axis=1).reshape(length, -1)
    values_in = hidden_in.astype(jnp.float32)
    middle = values_in + scatter_tokens(times(attn, rows_out))
    scale_two = inv_rms(middle)
    normed_two = gather_tokens((middle * scale_two * gain_two).astype(jnp.bfloat16))
    gate = times(normed_two, cols_gate)
    up = times(normed_two, cols_up)
    sig = jax.nn.sigmoid(gate)
    activated = gate * sig
    hid = (activated * up).astype(jnp.bfloat16)
    output = middle + scatter_tokens(times(hid, rows_down))
    g_down = scatter_rows(contract_rows(hid, cot_all))
    d_hid = times_trans(cot_all, rows_down)
    d_gate = (d_hid * up * sig * (1.0 + gate * (1.0 - sig))).astype(jnp.bfloat16)
    d_up = (d_hid * activated).astype(jnp.bfloat16)
    g_gate = scatter_cols(contract_rows(normed_two, d_gate))
    g_up = scatter_cols(contract_rows(normed_two, d_up))
    d_normed_two = scatter_tokens(times_trans(d_gate, cols_gate) + times_trans(d_up, cols_up))
    d_middle, part_two = norm_back(d_normed_two, middle, scale_two, gain_two)
    d_middle = cotangent.astype(jnp.float32) + d_middle
    d_low = gather_tokens(d_middle.astype(jnp.bfloat16))
    g_out = scatter_rows(contract_rows(attn, d_low))
    d_attn = times_trans(d_low, rows_out).astype(jnp.bfloat16)
    d_attn = d_attn.reshape(length, groups, 2, HEAD_DIM)
    pieces = []
    for g in range(groups):
        d_q, d_k, d_v = attend_backward(
            packed[:, g], forward[g][0], forward[g][1], d_attn[:, g], allowed, scale
        )
        turned = rotate(
            jnp.concatenate([d_q, d_k[:, None]], axis=1), cosine[:, None, :], -sine[:, None, :]
        )
        pieces.append(jnp.concatenate([turned, d_v[:, None]], axis=1))
    d_packed = jnp.stack(pieces, axis=1).reshape(length, -1).astype(jnp.bfloat16)
    g_qkv = scatter_cols(contract_rows(normed_one, d_packed))
    d_normed_one = scatter_tokens(times_trans(d_packed, cols_qkv))
    d_tokens, part_one = norm_back(d_normed_one, values_in, inv_rms(values_in), gain_one)
    d_tokens = d_middle + d_tokens
    g_gains = lax.psum_scatter(
        jnp.stack([part_one, part_two]), ("fsdp", "seq"), scatter_dimension=1, tiled=True
    )
    return (output, d_tokens, g_qkv, g_out, g_gate, g_up, g_down, g_gains[0], g_gains[1])


def solution(mesh):
    both = P(("fsdp", "seq"), None)
    split = P("fsdp", "seq")
    gain = P(("fsdp", "seq"))
    in_specs = (both, both, split, split, split, split, split, split, gain, gain)
    out_specs = (both, both, split, split, split, split, split, gain, gain)
    return jax.shard_map(body, mesh=mesh, in_specs=in_specs, out_specs=out_specs, check_vma=False)
```

profile of v0, /device:TPU:0, one launch (start us, length us, event | category | flops | bytes accessed | tf_op | source)
XLA Modules:
  0.0 949.5 jit_solution(4358844575518664176)
XLA Ops:
  7.2 1.6 collective-permute-start
  11.7 74.6 %all-gather.2 = bf16[32,48,2]{1,2,0:T(2,128)(2,1)S(1)} all-gather(bf16[1,48,2]{1,2,0:T(2,128)(2,1)S(1)} %maximum_bitcast_fusion.2), channel_id=1, replica_groups=mesh['fsdp'=8,'seq'=4] {'fsdp','seq'}, dimensions={0}, use_global_device_ids=true | all-gather | bytes 6336 | tf_op jit(solution)/shard_map/all_gather | solution.py:134
  86.4 7.2 all_gather.42
  96.3 2.6 copy.58
  100.0 2.6 fusion.12
  102.6 20.0 %all-gather.15.cloned.1.call-done = bf16[1536,768]{1,0:T(8,128)(2,1)} async-done(((bf16[192,768]{1,0:T(8,128)(2,1)}), bf16[1536,768]{1,0:T(8,128)(2,1)}) %all-gather.15.cloned.1.call-update) | async-done | bytes 2359312 | tf_op jit(solution)/shard_map/all_gather | solution.py:119
  122.6 5.5 fusion.69
  128.9 1.9 fusion.9
  130.8 4.1 exponential_reduce_fusion.1
  135.0 2.0 exponential_reduce_fusion
  138.3 2.9 fusion.44
  141.3 2.9 fusion.45
  145.2 3.5 convolution_convert_fusion.1
  151.8 47.1 %reduce-scatter.13.cloned.1.call-done = bf16[256,1536]{1,0:T(8,128)(2,1)} async-done(((bf16[1024,1536]{1,0:T(8,128)(2,1)}), bf16[256,1536]{1,0:T(8,128)(2,1)}) %reduce-scatter.13.cloned.1.call-update) | async-done | bytes 786448 | tf_op jit(solution)/shard_map/reduce_scatter | solution.py:130
  200.3 2.3 multiply_convert_fusion.3
  204.4 34.8 %all-gather.29.cloned.1.call-done = bf16[4096,384]{1,0:T(8,128)(2,1)} async-done(((bf16[512,384]{1,0:T(8,128)(2,1)}), bf16[4096,384]{1,0:T(8,128)(2,1)}) %all-gather.29.cloned.1.call-update) | async-done | bytes 3145744 | tf_op jit(solution)/shard_map/all_gather | solution.py:107
  239.2 4.3 copy.59
  243.5 2.2 copy.81
  245.8 32.1 %all-gather.21.cloned.1.call-done = bf16[1536,1024]{1,0:T(8,128)(2,1)} async-done(((bf16[192,1024]{1,0:T(8,128)(2,1)}), bf16[1536,1024]{1,0:T(8,128)(2,1)}) %all-gather.21.cloned.1.call-update) | async-done | bytes 3145744 | tf_op jit(solution)/shard_map/all_gather | solution.py:119
  277.9 45.3 %all-gather.17.cloned.1.call-done = bf16[1024,1536]{1,0:T(8,128)(2,1)} async-done(((bf16[256,1536]{1,0:T(8,128)(2,1)}), bf16[1024,1536]{1,0:T(8,128)(2,1)}) %all-gather.17.cloned.1.call-update) | async-done | bytes 3145744 | tf_op jit(solution)/shard_map/all_gather | solution.py:127
  323.2 8.3 fusion.95
  331.4 31.7 %all-gather.19.cloned.1.call-done = bf16[1536,1024]{1,0:T(8,128)(2,1)} async-done(((bf16[192,1024]{1,0:T(8,128)(2,1)}), bf16[1536,1024]{1,0:T(8,128)(2,1)}) %all-gather.19.cloned.1.call-update) | async-done | bytes 3145744 | tf_op jit(solution)/shard_map/all_gather | solution.py:119
  363.1 8.2 fusion.94
  371.4 36.5 %all-gather.23.cloned.1.call-done = bf16[1024,1536]{1,0:T(8,128)(2,1)} async-done(((bf16[256,1536]{1,0:T(8,128)(2,1)}), bf16[1024,1536]{1,0:T(8,128)(2,1)}) %all-gather.23.cloned.1.call-update) | async-done | bytes 3145744 | tf_op jit(solution)/shard_map/all_gather | solution.py:127
  407.8 11.6 %multiply_convert_fusion = (bf16[1024,1024]{1,0:T(8,128)(2,1)S(1)}, bf16[1024,1024]{1,0:T(8,128)(2,1)S(1)}, bf16[1024,1024]{1,0:T(8,128)(2,1)}) fusion(f32[1024,1024]{1,0:T(8,128)} %fusion.94, f32[1024,1024]{1,0:T(8,128)} %fusion.95, bf16[1024,1536]{1,0:T(8,128)(2,1)} %all-gather.23.cloned.1.call-done, bf16[1024,1536]{1,0:T(8,128)(2,1)} %bitcast.230), kind=kOutput, calls=%fused_computation.28 | convolution fusion | flops 3236954112 | bytes 20971520 | tf_op jit(solution)/shard_map/dot_general | solution.py:57
  419.4 3.9 fusion.96
  423.4 5.0 add_convert_fusion
  428.4 44.0 %reduce-scatter.17.cloned.1.call-done = bf16[256,1536]{1,0:T(8,128)(2,1)} async-done(((bf16[1024,1536]{1,0:T(8,128)(2,1)}), bf16[256,1536]{1,0:T(8,128)(2,1)}) %reduce-scatter.17.cloned.1.call-update) | async-done | bytes 786448 | tf_op jit(solution)/shard_map/reduce_scatter | solution.py:130
  472.5 2.4 fusion.36
  474.9 2.7 fusion.92
  477.7 7.6 convolution_convert_fusion.2
  485.3 6.3 reshape.273
  491.6 3.9 copy.67
  495.6 7.7 convolution_convert_fusion.3
  503.4 7.7 convolution_convert_fusion.4
  511.3 10.4 %all-gather.25.cloned.1.call-done = bf16[1024,1536]{1,0:T(8,128)(2,1)} async-done(((bf16[256,1536]{1,0:T(8,128)(2,1)}), bf16[1024,1536]{1,0:T(8,128)(2,1)}) %all-gather.25.cloned.1.call-update) | async-done | bytes 3145744 | tf_op jit(solution)/shard_map/all_gather | solution.py:127
  521.8 4.3 convolution_convert_fusion.7
  526.1 2.5 reshape.271
  529.8 3.8 convolution_convert_fusion.8
  534.0 5.4 fusion.3
  539.4 2.2 fusion.55
  541.6 3.1 fusion.1
  544.7 2.2 fusion.53
  547.8 1.8 fusion.42
  549.9 1.9 subtract_convert_fusion.2
  551.8 5.7 fusion.62
  557.7 5.7 fusion.65
  563.6 1.7 copy-done.9
  565.3 4.4 convolution_convert_fusion.6
  569.8 5.8 convolution_convert_fusion
  575.6 7.7 convolution_convert_fusion.5
  583.4 1.7 collective-permute-start.3
  585.7 42.7 %reduce-scatter.27.cloned.1.call-done = bf16[192,1024]{1,0:T(8,128)(2,1)} async-done(((bf16[1536,1024]{1,0:T(8,128)(2,1)}), bf16[192,1024]{1,0:T(8,128)(2,1)}) %reduce-scatter.27.cloned.1.call-update) | async-done | bytes 393232 | tf_op jit(solution)/shard_map/reduce_scatter | solution.py:122
  628.4 2.0 convert_element_type.187
  630.3 42.6 %reduce-scatter.25.cloned.1.call-done = bf16[192,1024]{1,0:T(8,128)(2,1)} async-done(((bf16[1536,1024]{1,0:T(8,128)(2,1)}), bf16[192,1024]{1,0:T(8,128)(2,1)}) %reduce-scatter.25.cloned.1.call-update) | async-done | bytes 393232 | tf_op jit(solution)/shard_map/reduce_scatter | solution.py:122
  673.0 2.0 convert_element_type.185
  674.9 32.4 %reduce-scatter.23.cloned.1.call-done = bf16[1,192,384]{2,1,0:T(8,128)(2,1)} async-done(((bf16[8,192,384]{2,1,0:T(8,128)(2,1)}), bf16[1,192,384]{2,1,0:T(8,128)(2,1)}) %reduce-scatter.23.cloned.1.call-update) | async-done | bytes 147472 | tf_op jit(solution)/shard_map/reduce_scatter | solution.py:115
  711.8 32.7 %reduce-scatter.21.cloned.1.call-done = bf16[192,768]{1,0:T(8,128)(2,1)} async-done(((bf16[1536,768]{1,0:T(8,128)(2,1)}), bf16[192,768]{1,0:T(8,128)(2,1)}) %reduce-scatter.21.cloned.1.call-update) | async-done | bytes 294928 | tf_op jit(solution)/shard_map/reduce_scatter | solution.py:122
  744.6 1.8 convert_element_type.181
  746.4 46.8 %reduce-scatter.19.cloned.1.call-done = bf16[256,1536]{1,0:T(8,128)(2,1)} async-done(((bf16[1024,1536]{1,0:T(8,128)(2,1)}), bf16[256,1536]{1,0:T(8,128)(2,1)}) %reduce-scatter.19.cloned.1.call-update) | async-done | bytes 786448 | tf_op jit(solution)/shard_map/reduce_scatter | solution.py:130
  793.2 1.6 fusion.41
  796.8 43.3 %reduce-scatter.15.cloned.1.call-done = bf16[256,1536]{1,0:T(8,128)(2,1)} async-done(((bf16[1024,1536]{1,0:T(8,128)(2,1)}), bf16[256,1536]{1,0:T(8,128)(2,1)}) %reduce-scatter.15.cloned.1.call-update) | async-done | bytes 786448 | tf_op jit(solution)/shard_map/reduce_scatter | solution.py:130
  840.1 4.1 fusion.31
  844.2 96.5 %reduce-scatter.31.cloned.1.call-done = f32[48,2]{1,0:T(8,128)} async-done(((f32[1536,2]{1,0:T(8,128)}), f32[48,2]{1,0:T(8,128)}) %reduce-scatter.31.cloned.1.call-update) | async-done | bytes 400
  (188 shorter events, 28.6 us)
Async XLA Ops:
  7.2 89.1 %all-gather.27.cloned.1.call-start = ((), (), s32[]{:S(2)}) async-start(), calls=%async_computation.26 | async-start | bytes 1327104 | tf_op jit(solution)/shard_map/all_gather | solution.py:107
  7.2 1.6 collective-permute-start
  9.5 90.5 %all-gather.13.cloned.1.call-start = ((), (), s32[]{:S(2)}) async-start(), calls=%async_computation.10 | async-start | bytes 3932160 | tf_op jit(solution)/shard_map/all_gather | solution.py:127
  10.2 112.4 %all-gather.15.cloned.1.call-start = ((), (), s32[]{:S(2)}) async-start(), calls=%async_computation.11 | async-start | bytes 2654208 | tf_op jit(solution)/shard_map/all_gather | solution.py:119
  11.0 187.9 %reduce-scatter.13.cloned.1.call-start = ((), (), s32[]{:S(2)}) async-start(), calls=%async_computation.12 | async-start | bytes 3932160 | tf_op jit(solution)/shard_map/reduce_scatter | solution.py:130
  95.6 32.6 %copy-start.13 = (f32[1024,48]{0,1:T(8,128)}, f32[1024,48]{0,1:T(8,128)S(1)}, u32[]{:S(2)}) copy-start(f32[1024,48]{0,1:T(8,128)S(1)} %get-tuple-element.39) | copy-start | bytes 589828
  96.2 45.0 %copy-start.6 = (pred[1024,1024]{0,1:T(8,128)(4,1)}, pred[1024,1024]{0,1:T(8,128)(4,1)S(1)}, u32[]{:S(2)}) copy-start(pred[1024,1024]{0,1:T(8,128)(4,1)S(1)} %fusion.22) | copy-start | bytes 3145732
  102.6 25.6 %copy-start.42 = (f32[1024]{0:T(1024)}, f32[1024]{0:T(1024)S(1)}, u32[]{:S(2)}) copy-start(f32[1024]{0:T(1024)S(1)} %add_rsqrt_fusion) | copy-start | bytes 12292
  128.9 12.3 %copy-start.11 = (bf16[1024,4,96]{0,2,1:T(8,128)(2,1)}, bf16[1024,4,96]{0,2,1:T(8,128)(2,1)S(1)}, u32[]{:S(2)}) copy-start(bf16[1024,4,96]{0,2,1:T(8,128)(2,1)S(1)} %get-tuple-element.31) | copy-start | bytes 2359300
  128.9 415.8 %copy-start.10 = (bf16[1024,4,96]{0,2,1:T(8,128)(2,1)}, bf16[1024,4,96]{0,2,1:T(8,128)(2,1)S(1)}, u32[]{:S(2)}) copy-start(bf16[1024,4,96]{0,2,1:T(8,128)(2,1)S(1)} %get-tuple-element.32) | copy-start | bytes 2359300
  130.8 10.4 %copy-start.47 = (f32[1024,1024,2]{1,0,2:T(8,128)}, f32[1024,1024,2]{1,0,2:T(8,128)S(1)}, u32[]{:S(2)}) copy-start(f32[1024,1024,2]{1,0,2:T(8,128)S(1)} %get-tuple-element.45) | copy-start | bytes 25165828
  135.0 3.3 copy-start.2
  137.0 4.2 copy-start.35
  137.0 4.2 copy-start.38
  141.2 3.0 copy-start.15
  141.3 4.0 copy-start.19
  144.2 4.5 copy-start.17
  148.7 50.1 %copy-start = (bf16[256,1536]{1,0:T(8,128)(2,1)S(1)}, bf16[256,1536]{1,0:T(8,128)(2,1)}, u32[]{:S(2)}) copy-start(bf16[256,1536]{1,0:T(8,128)(2,1)} %param.10) | copy-start | bytes 2359300
  148.7 90.5 %all-gather.29.cloned.1.call-start = ((), (), s32[]{:S(2)}) async-start(), calls=%async_computation.27 | async-start | bytes 3538944 | tf_op jit(solution)/shard_map/all_gather | solution.py:107
  149.7 0.7 collective-permute-start.1
  151.2 126.7 %all-gather.21.cloned.1.call-start = ((), (), s32[]{:S(2)}) async-start(), calls=%async_computation.15 | async-start | bytes 3538944 | tf_op jit(solution)/shard_map/all_gather | solution.py:119
  151.7 171.4 %all-gather.17.cloned.1.call-start = ((), (), s32[]{:S(2)}) async-start(), calls=%async_computation.13 | async-start | bytes 3932160 | tf_op jit(solution)/shard_map/all_gather | solution.py:127
  200.3 274.6 %copy-start.28 = (f32[256]{0:T(256)}, f32[256]{0:T(256)S(1)}, u32[]{:S(2)}) copy-start(f32[256]{0:T(256)S(1)} %get-tuple-element.43) | copy-start | bytes 3076
  200.3 274.6 %copy-start.31 = (f32[256]{0:T(256)}, f32[256]{0:T(256)S(1)}, u32[]{:S(2)}) copy-start(f32[256]{0:T(256)S(1)} %get-tuple-element.42) | copy-start | bytes 3076
  202.7 160.5 %all-gather.19.cloned.1.call-start = ((), (), s32[]{:S(2)}) async-start(), calls=%async_computation.14 | async-start | bytes 3538944 | tf_op jit(solution)/shard_map/all_gather | solution.py:119
  203.4 204.4 %all-gather.23.cloned.1.call-start = ((), (), s32[]{:S(2)}) async-start(), calls=%async_computation.17 | async-start | bytes 3932160 | tf_op jit(solution)/shard_map/all_gather | solution.py:127
  204.2 268.3 %reduce-scatter.17.cloned.1.call-start = ((), (), s32[]{:S(2)}) async-start(), calls=%async_computation.18 | async-start | bytes 3932160 | tf_op jit(solution)/shard_map/reduce_scatter | solution.py:130
  407.8 11.6 %copy-start.45 = (bf16[1536,1024]{1,0:T(8,128)(2,1)S(1)}, bf16[1536,1024]{1,0:T(8,128)(2,1)}, u32[]{:S(2)}) copy-start(bf16[1536,1024]{1,0:T(8,128)(2,1)} %all-gather.19.cloned.1.call-done) | copy-start | bytes 9437188
  419.4 3.9 copy-start.48
  419.4 3.9 copy-start.49
  419.4 3.9 copy-start.44
  428.4 44.1 %copy-start.1 = (bf16[256,1536]{1,0:T(8,128)(2,1)S(1)}, bf16[256,1536]{1,0:T(8,128)(2,1)}, u32[]{:S(2)}) copy-start(bf16[256,1536]{1,0:T(8,128)(2,1)} %reduce-scatter.13.cloned.1.call-done) | copy-start | bytes 2359300
  428.4 46.6 %copy-start.3 = (bf16[256,1536]{1,0:T(8,128)(2,1)S(1)}, bf16[256,1536]{1,0:T(8,128)(2,1)}, u32[]{:S(2)}) copy-start(bf16[256,1536]{1,0:T(8,128)(2,1)} %param.11) | copy-start | bytes 2359300
  428.4 93.4 %all-gather.25.cloned.1.call-start = ((), (), s32[]{:S(2)}) async-start(), calls=%async_computation.19 | async-start | bytes 3932160 | tf_op jit(solution)/shard_map/all_gather | solution.py:127
  474.9 10.4 %copy-start.33 = (f32[256]{0:T(256)}, f32[256]{0:T(256)S(1)}, u32[]{:S(2)}) copy-start(f32[256]{0:T(256)S(1)} %broadcast_multiply_fusion.1) | copy-start | bytes 3076
  477.7 105.7 %reduce-scatter.29.cloned.1.call-start = ((), (), s32[]{:S(2)}) async-start(), calls=%async_computation.25 | async-start | bytes 3538944 | tf_op jit(solution)/shard_map/reduce_scatter | solution.py:115
  495.6 132.8 %reduce-scatter.27.cloned.1.call-start = ((), (), s32[]{:S(2)}) async-start(), calls=%async_computation.24 | async-start | bytes 3538944 | tf_op jit(solution)/shard_map/reduce_scatter | solution.py:122
  503.3 169.6 %reduce-scatter.25.cloned.1.call-start = ((), (), s32[]{:S(2)}) async-start(), calls=%async_computation.23 | async-start | bytes 3538944 | tf_op jit(solution)/shard_map/reduce_scatter | solution.py:122
  511.1 10.7 %copy-start.21 = (bf16[1024,2,2,96]{0,3,2,1:T(8,128)(2,1)S(1)}, bf16[1024,2,2,96]{0,3,2,1:T(8,128)(2,1)}, u32[]{:S(2)}) copy-start(bf16[1024,2,2,96]{0,3,2,1:T(8,128)(2,1)} %copy-done.20) | copy-start | bytes 2359300
  511.1 196.2 %reduce-scatter.23.cloned.1.call-start = ((), (), s32[]{:S(2)}) async-start(), calls=%async_computation.22 | async-start | bytes 1327104 | tf_op jit(solution)/shard_map/reduce_scatter | solution.py:115
  529.8 3.9 copy-start.16
  529.8 3.9 copy-start.18
  529.8 4.2 copy-start.7
  529.8 4.2 copy-start.12
  529.8 4.2 copy-start.39
  529.8 11.8 %slice-start = ((s8[8388608]{0:T(1024)(128)(4,1)}), s8[4194304]{0:T(1024)(128)(4,1)S(1)}, s32[]{:S(2)}) async-start(s8[8388608]{0:T(1024)(128)(4,1)} %bitcast.225), calls=%async_computation.29 | async-start | bytes 8388608
  533.6 7.9 copy-start.22
  534.0 7.6 slice-start.1
  539.4 2.2 copy-start.36
  547.7 2.2 copy-start.24
  549.6 195.0 %reduce-scatter.21.cloned.1.call-start = ((), (), s32[]{:S(2)}) async-start(), calls=%async_computation.21 | async-start | bytes 2654208 | tf_op jit(solution)/shard_map/reduce_scatter | solution.py:122
  551.8 5.8 copy-start.37
  569.8 223.5 %reduce-scatter.19.cloned.1.call-start = ((), (), s32[]{:S(2)}) async-start(), calls=%async_computation.20 | async-start | bytes 3932160 | tf_op jit(solution)/shard_map/reduce_scatter | solution.py:130
  575.6 264.5 %reduce-scatter.15.cloned.1.call-start = ((), (), s32[]{:S(2)}) async-start(), calls=%async_computation.16 | async-start | bytes 3932160 | tf_op jit(solution)/shard_map/reduce_scatter | solution.py:130
  583.3 357.4 %reduce-scatter.31.cloned.1.call-start = ((), (), s32[]{:S(2)}) async-start(), calls=%async_computation.28 | async-start | bytes 811008
  583.4 126.7 %collective-permute-start.3 = (bf16[512,384]{1,0:T(8,128)(2,1)}, bf16[512,384]{1,0:T(8,128)(2,1)S(1)}, u32[]{:S(2)}, u32[]{:S(2)}) collective-permute-start(bf16[512,384]{1,0:T(8,128)(2,1)} %bitcast.258), channel_id=1, source_target_pairs={{0,0},{4,1},{8,2},{12,3},{16,4},{20,5},{24,6},{28,7},{1,8},{5,9},{... | collective-permute-start | bytes 1179656 | tf_op jit(solution)/shard_map/ppermute | solution.py:116
  674.9 165.1 %copy-start.4 = (bf16[256,1536]{1,0:T(8,128)(2,1)S(1)}, bf16[256,1536]{1,0:T(8,128)(2,1)}, u32[]{:S(2)}) copy-start(bf16[256,1536]{1,0:T(8,128)(2,1)} %param.11) | copy-start | bytes 2359300
  674.9 165.1 %copy-start.5 = (bf16[256,1536]{1,0:T(8,128)(2,1)S(1)}, bf16[256,1536]{1,0:T(8,128)(2,1)}, u32[]{:S(2)}) copy-start(bf16[256,1536]{1,0:T(8,128)(2,1)} %reduce-scatter.17.cloned.1.call-done) | copy-start | bytes 2359300
  707.3 3.8 collective-permute-start.2
  711.1 129.0 %copy-start.29 = (f32[256]{0:T(256)S(1)}, f32[256]{0:T(256)}, u32[]{:S(2)}) copy-start(f32[256]{0:T(256)} %copy-done.28) | copy-start | bytes 3076
  711.1 129.0 %copy-start.30 = (f32[256]{0:T(256)S(1)}, f32[256]{0:T(256)}, u32[]{:S(2)}) copy-start(f32[256]{0:T(256)} %get-tuple-element.41) | copy-start | bytes 3076
  711.1 129.0 %copy-start.32 = (f32[256]{0:T(256)S(1)}, f32[256]{0:T(256)}, u32[]{:S(2)}) copy-start(f32[256]{0:T(256)} %copy-done.31) | copy-start | bytes 3076
  711.1 129.0 %copy-start.34 = (f32[256]{0:T(256)S(1)}, f32[256]{0:T(256)}, u32[]{:S(2)}) copy-start(f32[256]{0:T(256)} %copy-done.33) | copy-start | bytes 3076
  711.1 129.0 %copy-start.41 = (f32[256]{0:T(256)S(1)}, f32[256]{0:T(256)}, u32[]{:S(2)}) copy-start(f32[256]{0:T(256)} %get-tuple-element.40) | copy-start | bytes 3076
  (11 other events, 16.9 us)
Sparse Core Ops, SparseCore 0:
  10.2 33.3 all-gather.26
  45.4 43.8 all-gather.12
  91.0 31.6 all-gather.14
  148.8 49.9 reduce-scatter.12
  200.9 38.2 all-gather.28
  240.7 37.1 all-gather.20
  280.3 42.8 all-gather.16
  324.8 38.2 all-gather.18
  365.0 42.8 all-gather.22
  428.5 43.9 reduce-scatter.16
  477.8 43.9 all-gather.24
  523.9 40.3 reduce-scatter.28
  566.6 61.7 reduce-scatter.26
  630.5 42.3 reduce-scatter.24
  675.7 31.6 reduce-scatter.22
  709.5 35.0 reduce-scatter.20
  747.4 45.7 reduce-scatter.18
  796.1 43.9 reduce-scatter.14
  845.2 95.4 reduce-scatter.30
where the time goes:
time: 960 us; the launch traced here: 950 us
  waiting for transfers between devices  643 us (67%)
  matrix products  134 us (14%)
  blocking collectives  81.8 us (9%)
  other arithmetic  34.8 us (4%)
  local copies, waits for them, and re-layouts  34.7 us (4%)
  between operations  15 us (2%)
    reduce_scatter x4, waiting for transfers between devices, scatter_tokens(): lax.psum_scatter(partial.astype(jnp.bfloat16), 'seq', scatter_dimension=0...  181 us
    reduce_scatter x3, waiting for transfers between devices, scatter_cols(): lax.psum_scatter(grad.astype(jnp.bfloat16), 'fsdp', scatter_dimension=0,...  118 us
    unnamed x20, waiting for transfers between devices  100 us
    all_gather x4, waiting for transfers between devices, gather_tokens(): return lax.all_gather(block, 'seq', axis=0, tiled=True)  92.2 us
    all_gather x3, waiting for transfers between devices, gather_cols(): return lax.all_gather(shard, 'fsdp', axis=0, tiled=True)  83.8 us
    all_gather x1, blocking collectives, body(): lax.all_gather(jnp.stack([gain_attn, gain_mlp]), ('fsdp', 'seq'), axis=1,...  74.6 us
    all_gather x2, waiting for transfers between devices, gather_rows(): blocks = lax.all_gather(moved, 'fsdp', axis=0, tiled=False)  34.9 us
    dot_general x5, matrix products, times(): return jnp.dot(left, right, preferred_element_type=jnp.float32)  33.2 us
  transfers between devices with their start and end apart: 23, of which 16 were waited for; matrix products, arithmetic and copies ran while one was open for 15% of the time, Pallas kernels for 0%

commit v1 on v0

--- a/solution.py
+++ b/solution.py
@@ -8,6 +8,19 @@
 EPSILON = 1e-05
 ROPE_BASE = 100000.0
 NEGATIVE = -1e30
+
+
+def gather_around(x, axis, dim):
+    ways = lax.axis_size(axis)
+    up = [(d, (d + 1) % ways) for d in range(ways)]
+    down = [(d, (d - 1) % ways) for d in range(ways)]
+    earlier, later = ([x], [x])
+    for _ in range(ways // 2):
+        earlier.append(lax.ppermute(earlier[-1], axis, up))
+    for _ in range((ways - 1) // 2):
+        later.append(lax.ppermute(later[-1], axis, down))
+    line = jnp.concatenate([*earlier[::-1], *later[1:]], axis=dim)
+    return jnp.roll(line, (lax.axis_index(axis) - ways // 2) * x.shape[dim], axis=dim)
 
 
 def rope_tables(ids):
@@ -116,7 +129,7 @@
         return lax.ppermute(own, ("fsdp", "seq"), back).astype(jnp.float32)
 
     def gather_cols(shard):
-        return lax.all_gather(shard, "fsdp", axis=0, tiled=True)
+        return gather_around(shard, "fsdp", 0)
 
     def scatter_cols(grad):
         return lax.psum_scatter(

time: 960 us -> 922 us (0.960)
  waiting for transfers between devices: 643 us -> 553 us
  starting transfers between devices: 6.78 us -> 54.9 us
  local copies, waits for them, and re-layouts: 34.7 us -> 54.3 us
    all_gather x3 -> x0, waiting for transfers between devices: 83.8 us -> none  [gather_cols(): return lax.all_gather(shard, 'fsdp', axis=0, tiled=True)]
    ppermute x0 -> x21, waiting for transfers between devices: none -> 78 us  [the longest x12 72.1 us: gather_around(): earlier.append(lax.ppermute(earlier[-1], axis, up))]
    ppermute x0 -> x21, starting transfers between devices: none -> 47.9 us  [the longest x9 34.9 us: gather_around(): later.append(lax.ppermute(later[-1], axis, down))]
    all_gather x4, waiting for transfers between devices: 92.2 us -> 47.5 us  [gather_tokens(): return lax.all_gather(block, 'seq', axis=0, tiled=True)]
    all_gather x2, waiting for transfers between devices: 34.9 us -> 0.01 us  [gather_rows(): blocks = lax.all_gather(moved, 'fsdp', axis=0, tiled=False)]
    unnamed x109 -> x152, local copies, waits for them, and re-layouts: 12.2 us -> 30.6 us
    unnamed x20 -> x17, waiting for transfers between devices: 100 us -> 97.8 us
  transfers between devices with their start and end apart: 23 -> 41, of which waited for: 16 -> 24; matrix products, arithmetic and copies ran while one was open for 15% -> 17% of each run, Pallas kernels for 0% -> 0%
where the time goes in v1:
time: 922 us; the launch traced here: 917 us
  waiting for transfers between devices  553 us (60%)
  matrix products  132 us (14%)
  blocking collectives  72.3 us (8%)
  starting transfers between devices  54.9 us (6%)
  local copies, waits for them, and re-layouts  54.3 us (6%)
  other arithmetic  35.7 us (4%)
  between operations  15.2 us (2%)
    reduce_scatter x4, waiting for transfers between devices, scatter_tokens(): lax.psum_scatter(partial.astype(jnp.bfloat16), 'seq', scatter_dimension=0...  178 us
    reduce_scatter x3, waiting for transfers between devices, scatter_cols(): lax.psum_scatter(grad.astype(jnp.bfloat16), 'fsdp', scatter_dimension=0,...  118 us
    unnamed x17, waiting for transfers between devices  97.8 us
    ppermute x12, waiting for transfers between devices, gather_around(): earlier.append(lax.ppermute(earlier[-1], axis, up))  72.1 us
    all_gather x1, blocking collectives, body(): lax.all_gather(jnp.stack([gain_attn, gain_mlp]), ('fsdp', 'seq'), axis=1,...  66.1 us
    all_gather x4, waiting for transfers between devices, gather_tokens(): return lax.all_gather(block, 'seq', axis=0, tiled=True)  47.5 us
    ppermute x9, starting transfers between devices, gather_around(): later.append(lax.ppermute(later[-1], axis, down))  34.9 us
    reduce_scatter x2, waiting for transfers between devices, scatter_rows(): own = lax.psum_scatter(blocks, 'fsdp', scatter_dimension=0, tiled=False)  32.7 us
  transfers between devices with their start and end apart: 41, of which 24 were waited for; matrix products, arithmetic and copies ran while one was open for 17% of the time, Pallas kernels for 0%

profile of v1, /device:TPU:0, one launch (start us, length us, event | category | flops | bytes accessed | tf_op | source)
XLA Modules:
  0.0 917.5 jit_solution(246414644441899815)
XLA Ops:
  10.4 6.9 collective-permute-start
  17.4 7.4 collective-permute-start.4
  25.4 66.1 %all-gather.2 = bf16[32,48,2]{1,2,0:T(2,128)(2,1)S(1)} all-gather(bf16[1,48,2]{1,2,0:T(2,128)(2,1)S(1)} %maximum_bitcast_fusion.2), channel_id=1, replica_groups=mesh['fsdp'=8,'seq'=4] {'fsdp','seq'}, dimensions={0}, use_global_device_ids=true | all-gather | bytes 6336 | tf_op jit(solution)/shard_map/all_gather | solution.py:147
  91.6 6.3 all_gather.32
  98.5 8.0 collective-permute-done.1
  108.0 3.5 collective-permute-start.5
  111.5 3.9 collective-permute-done.2
  116.1 4.1 collective-permute-start.6
  120.1 3.9 collective-permute-done.3
  139.2 2.7 fusion.12
  142.1 4.7 fusion.30
  149.4 3.7 exponential_reduce_fusion.1
  156.5 2.9 fusion.49
  159.4 2.9 fusion.50
  163.4 3.5 convolution_convert_fusion.1
  170.1 44.7 %reduce-scatter.13.cloned.1.call-done = bf16[256,1536]{1,0:T(8,128)(2,1)} async-done(((bf16[1024,1536]{1,0:T(8,128)(2,1)}), bf16[256,1536]{1,0:T(8,128)(2,1)}) %reduce-scatter.13.cloned.1.call-update) | async-done | bytes 786448 | tf_op jit(solution)/shard_map/reduce_scatter | solution.py:143
  216.8 2.3 multiply_convert_fusion.3
  220.9 7.5 collective-permute-done.15
  228.4 3.5 collective-permute-start.12
  232.0 9.4 %collective-permute-done.8 = bf16[192,1024]{1,0:T(8,128)(2,1)S(1)} collective-permute-done((bf16[192,1024]{1,0:T(8,128)(2,1)S(1)}, bf16[192,1024]{1,0:T(8,128)(2,1)S(1)}, u32[]{:S(2)}, u32[]{:S(2)}) %collective-permute-start.8) | collective-permute-done | bytes 393248 | tf_op jit(solution)/shard_map/ppermute | solution.py:19
  241.4 16.8 %collective-permute-done.16 = bf16[192,1024]{1,0:T(8,128)(2,1)S(1)} collective-permute-done((bf16[192,1024]{1,0:T(8,128)(2,1)S(1)}, bf16[192,1024]{1,0:T(8,128)(2,1)S(1)}, u32[]{:S(2)}, u32[]{:S(2)}) %collective-permute-start.16) | collective-permute-done | bytes 393248 | tf_op jit(solution)/shard_map/ppermute | solution.py:19
  258.3 3.5 collective-permute-start.13
  261.8 4.9 collective-permute-done.19
  266.7 5.7 collective-permute-start.20
  273.2 2.3 collective-permute-start.10
  275.5 6.7 collective-permute-done.17
  282.4 3.4 collective-permute-start.14
  286.7 3.7 collective-permute-start.21
  292.5 6.5 collective-permute-done.18
  299.2 8.3 collective-permute-done.11
  315.5 4.3 copy.59
  322.1 8.3 fusion.107
  330.4 37.1 %all-gather.12.cloned.1.call-done = bf16[1024,1536]{1,0:T(8,128)(2,1)} async-done(((bf16[256,1536]{1,0:T(8,128)(2,1)}), bf16[1024,1536]{1,0:T(8,128)(2,1)}) %all-gather.12.cloned.1.call-update) | async-done | bytes 3145744 | tf_op jit(solution)/shard_map/all_gather | solution.py:140
  367.5 6.8 fusion.102
  374.3 8.3 multiply_convert_fusion.1
  382.6 4.4 fusion.104
  387.0 9.1 add_convert_fusion
  396.6 43.7 %reduce-scatter.17.cloned.1.call-done = bf16[256,1536]{1,0:T(8,128)(2,1)} async-done(((bf16[1024,1536]{1,0:T(8,128)(2,1)}), bf16[256,1536]{1,0:T(8,128)(2,1)}) %reduce-scatter.17.cloned.1.call-update) | async-done | bytes 786448 | tf_op jit(solution)/shard_map/reduce_scatter | solution.py:143
  440.3 2.4 fusion.41
  442.7 2.7 fusion.98
  445.5 7.7 convolution_convert_fusion.2
  453.2 6.2 reshape.273
  459.5 4.0 copy.67
  463.6 7.6 convolution_convert_fusion.4
  471.4 7.7 convolution_convert_fusion.3
  479.2 10.4 %all-gather.16.cloned.1.call-done = bf16[1024,1536]{1,0:T(8,128)(2,1)} async-done(((bf16[256,1536]{1,0:T(8,128)(2,1)}), bf16[1024,1536]{1,0:T(8,128)(2,1)}) %all-gather.16.cloned.1.call-update) | async-done | bytes 3145744 | tf_op jit(solution)/shard_map/all_gather | solution.py:140
  489.6 4.3 convolution_convert_fusion.7
  493.9 2.5 reshape.271
  497.6 3.8 convolution_convert_fusion.8
  501.8 5.4 fusion.3
  509.4 3.2 fusion.1
  519.7 5.7 fusion.67
  525.5 5.7 fusion.70
  533.2 4.4 convolution_convert_fusion.6
  537.7 5.8 convolution_convert_fusion
  543.5 7.6 convolution_convert_fusion.5
  553.5 42.7 %reduce-scatter.25.cloned.1.call-done = bf16[192,1024]{1,0:T(8,128)(2,1)} async-done(((bf16[1536,1024]{1,0:T(8,128)(2,1)}), bf16[192,1024]{1,0:T(8,128)(2,1)}) %reduce-scatter.25.cloned.1.call-update) | async-done | bytes 393232 | tf_op jit(solution)/shard_map/reduce_scatter | solution.py:135
  598.2 42.8 %reduce-scatter.27.cloned.1.call-done = bf16[192,1024]{1,0:T(8,128)(2,1)} async-done(((bf16[1536,1024]{1,0:T(8,128)(2,1)}), bf16[192,1024]{1,0:T(8,128)(2,1)}) %reduce-scatter.27.cloned.1.call-update) | async-done | bytes 393232 | tf_op jit(solution)/shard_map/reduce_scatter | solution.py:135
  642.9 32.7 %reduce-scatter.23.cloned.1.call-done = bf16[1,192,384]{2,1,0:T(8,128)(2,1)} async-done(((bf16[8,192,384]{2,1,0:T(8,128)(2,1)}), bf16[1,192,384]{2,1,0:T(8,128)(2,1)}) %reduce-scatter.23.cloned.1.call-update) | async-done | bytes 147472 | tf_op jit(solution)/shard_map/reduce_scatter | solution.py:128
  680.1 32.6 %reduce-scatter.21.cloned.1.call-done = bf16[192,768]{1,0:T(8,128)(2,1)} async-done(((bf16[1536,768]{1,0:T(8,128)(2,1)}), bf16[192,768]{1,0:T(8,128)(2,1)}) %reduce-scatter.21.cloned.1.call-update) | async-done | bytes 294928 | tf_op jit(solution)/shard_map/reduce_scatter | solution.py:135
  714.5 46.8 %reduce-scatter.19.cloned.1.call-done = bf16[256,1536]{1,0:T(8,128)(2,1)} async-done(((bf16[1024,1536]{1,0:T(8,128)(2,1)}), bf16[256,1536]{1,0:T(8,128)(2,1)}) %reduce-scatter.19.cloned.1.call-update) | async-done | bytes 786448 | tf_op jit(solution)/shard_map/reduce_scatter | solution.py:143
  764.9 43.3 %reduce-scatter.15.cloned.1.call-done = bf16[256,1536]{1,0:T(8,128)(2,1)} async-done(((bf16[1024,1536]{1,0:T(8,128)(2,1)}), bf16[256,1536]{1,0:T(8,128)(2,1)}) %reduce-scatter.15.cloned.1.call-update) | async-done | bytes 786448 | tf_op jit(solution)/shard_map/reduce_scatter | solution.py:143
  808.2 4.1 fusion.36
  812.3 96.4 %reduce-scatter.31.cloned.1.call-done = f32[48,2]{1,0:T(8,128)} async-done(((f32[1536,2]{1,0:T(8,128)}), f32[48,2]{1,0:T(8,128)}) %reduce-scatter.31.cloned.1.call-update) | async-done | bytes 400
  (267 shorter events, 81.9 us)
Async XLA Ops:
  7.2 119.8 %copy-start.21 = (bf16[192,768]{1,0:T(8,128)(2,1)S(1)}, bf16[192,768]{1,0:T(8,128)(2,1)}, u32[]{:S(2)}) copy-start(bf16[192,768]{1,0:T(8,128)(2,1)} %param.15) | copy-start | bytes 884740
  7.2 128.7 %all-gather.18.cloned.1.call-start = ((), (), s32[]{:S(2)}) async-start(), calls=%async_computation.23 | async-start | bytes 1327104 | tf_op jit(solution)/shard_map/all_gather | solution.py:120
  7.2 1.7 collective-permute-start.7
  9.6 129.6 %all-gather.10.cloned.1.call-start = ((), (), s32[]{:S(2)}) async-start(), calls=%async_computation.10 | async-start | bytes 3932160 | tf_op jit(solution)/shard_map/all_gather | solution.py:140
  10.4 204.4 %reduce-scatter.13.cloned.1.call-start = ((), (), s32[]{:S(2)}) async-start(), calls=%async_computation.11 | async-start | bytes 3932160 | tf_op jit(solution)/shard_map/reduce_scatter | solution.py:143
  10.4 87.9 %collective-permute-start = (bf16[192,768]{1,0:T(8,128)(2,1)}, bf16[192,768]{1,0:T(8,128)(2,1)S(1)}, u32[]{:S(2)}, u32[]{:S(2)}) collective-permute-start(bf16[192,768]{1,0:T(8,128)(2,1)} %param.15), channel_id=1, source_target_pairs={{0,4},{4,8},{8,12},{12,16},{16,20},{20,24},{24,28},{28,0},{1,5},{5... | collective-permute-start | bytes 884744 | tf_op jit(solution)/shard_map/ppermute | solution.py:19
  17.4 90.6 %collective-permute-start.4 = (bf16[192,768]{1,0:T(8,128)(2,1)}, bf16[192,768]{1,0:T(8,128)(2,1)S(1)}, u32[]{:S(2)}, u32[]{:S(2)}) collective-permute-start(bf16[192,768]{1,0:T(8,128)(2,1)} %param.15), channel_id=1, source_target_pairs={{0,28},{4,0},{8,4},{12,8},{16,12},{20,16},{24,20},{28,24},{1,29},{... | collective-permute-start | bytes 884744 | tf_op jit(solution)/shard_map/ppermute | solution.py:21
  98.3 8.1 collective-permute-start.1
  106.5 8.9 collective-permute-start.2
  108.0 38.9 %copy-start.14 = (f32[1024,48]{0,1:T(8,128)}, f32[1024,48]{0,1:T(8,128)S(1)}, u32[]{:S(2)}) copy-start(f32[1024,48]{0,1:T(8,128)S(1)} %get-tuple-element.40) | copy-start | bytes 589828
  108.0 8.1 collective-permute-start.5
  115.4 8.6 collective-permute-start.3
  116.0 43.3 %copy-start.6 = (pred[1024,1024]{0,1:T(8,128)(4,1)}, pred[1024,1024]{0,1:T(8,128)(4,1)S(1)}, u32[]{:S(2)}) copy-start(pred[1024,1024]{0,1:T(8,128)(4,1)S(1)} %fusion.22) | copy-start | bytes 3145732
  116.1 13.2 %collective-permute-start.6 = (bf16[192,768]{1,0:T(8,128)(2,1)S(1)}, bf16[192,768]{1,0:T(8,128)(2,1)S(1)}, u32[]{:S(2)}, u32[]{:S(2)}) collective-permute-start(bf16[192,768]{1,0:T(8,128)(2,1)S(1)} %collective-permute-done.5), channel_id=1, source_target_pairs={{0,28},{4,0},{8,4},{12,8},{16,12},{20,16},{24,20},{28,24},{1,29},{... | collective-permute-start | bytes 884744 | tf_op jit(solution)/shard_map/ppermute | solution.py:21
  147.5 11.9 %copy-start.12 = (bf16[1024,4,96]{0,2,1:T(8,128)(2,1)}, bf16[1024,4,96]{0,2,1:T(8,128)(2,1)S(1)}, u32[]{:S(2)}) copy-start(bf16[1024,4,96]{0,2,1:T(8,128)(2,1)S(1)} %get-tuple-element.32) | copy-start | bytes 2359300
  147.5 365.1 %copy-start.11 = (bf16[1024,4,96]{0,2,1:T(8,128)(2,1)}, bf16[1024,4,96]{0,2,1:T(8,128)(2,1)S(1)}, u32[]{:S(2)}) copy-start(bf16[1024,4,96]{0,2,1:T(8,128)(2,1)S(1)} %get-tuple-element.33) | copy-start | bytes 2359300
  149.4 10.0 %copy-start.53 = (f32[1024,1024,2]{1,0,2:T(8,128)}, f32[1024,1024,2]{1,0,2:T(8,128)S(1)}, u32[]{:S(2)}) copy-start(f32[1024,1024,2]{1,0,2:T(8,128)S(1)} %get-tuple-element.46) | copy-start | bytes 25165828
  166.9 47.9 %copy-start = (bf16[256,1536]{1,0:T(8,128)(2,1)S(1)}, bf16[256,1536]{1,0:T(8,128)(2,1)}, u32[]{:S(2)}) copy-start(bf16[256,1536]{1,0:T(8,128)(2,1)} %param.12) | copy-start | bytes 2359300
  166.9 52.3 %copy-start.27 = (bf16[192,1024]{1,0:T(8,128)(2,1)S(1)}, bf16[192,1024]{1,0:T(8,128)(2,1)}, u32[]{:S(2)}) copy-start(bf16[192,1024]{1,0:T(8,128)(2,1)} %param.18) | copy-start | bytes 1179652
  166.9 52.4 %copy-start.28 = (bf16[192,1024]{1,0:T(8,128)(2,1)S(1)}, bf16[192,1024]{1,0:T(8,128)(2,1)}, u32[]{:S(2)}) copy-start(bf16[192,1024]{1,0:T(8,128)(2,1)} %param.17) | copy-start | bytes 1179652
  166.9 148.6 %all-gather.20.cloned.1.call-start = ((), (), s32[]{:S(2)}) async-start(), calls=%async_computation.24 | async-start | bytes 3538944 | tf_op jit(solution)/shard_map/all_gather | solution.py:120
  168.0 0.7 collective-permute-start.22
  169.4 152.6 %all-gather.14.cloned.1.call-start = ((), (), s32[]{:S(2)}) async-start(), calls=%async_computation.14 | async-start | bytes 3932160 | tf_op jit(solution)/shard_map/all_gather | solution.py:140
  170.0 197.5 %all-gather.12.cloned.1.call-start = ((), (), s32[]{:S(2)}) async-start(), calls=%async_computation.12 | async-start | bytes 3932160 | tf_op jit(solution)/shard_map/all_gather | solution.py:140
  219.2 221.1 %reduce-scatter.17.cloned.1.call-start = ((), (), s32[]{:S(2)}) async-start(), calls=%async_computation.15 | async-start | bytes 3932160 | tf_op jit(solution)/shard_map/reduce_scatter | solution.py:143
  219.2 9.2 collective-permute-start.15
  219.3 22.1 %collective-permute-start.8 = (bf16[192,1024]{1,0:T(8,128)(2,1)S(1)}, bf16[192,1024]{1,0:T(8,128)(2,1)S(1)}, u32[]{:S(2)}, u32[]{:S(2)}) collective-permute-start(bf16[192,1024]{1,0:T(8,128)(2,1)S(1)} %copy-done.28), channel_id=1, source_target_pairs={{0,4},{4,8},{8,12},{12,16},{16,20},{20,24},{24,28},{28,0},{1,5},{5... | collective-permute-start | bytes 1179656 | tf_op jit(solution)/shard_map/ppermute | solution.py:19
  228.4 29.9 %collective-permute-start.16 = (bf16[192,1024]{1,0:T(8,128)(2,1)S(1)}, bf16[192,1024]{1,0:T(8,128)(2,1)S(1)}, u32[]{:S(2)}, u32[]{:S(2)}) collective-permute-start(bf16[192,1024]{1,0:T(8,128)(2,1)S(1)} %collective-permute-done.15), channel_id=1, source_target_pairs={{0,4},{4,8},{8,12},{12,16},{16,20},{20,24},{24,28},{28,0},{1,5},{5... | collective-permute-start | bytes 1179656 | tf_op jit(solution)/shard_map/ppermute | solution.py:19
  228.4 29.9 %collective-permute-start.12 = (bf16[192,1024]{1,0:T(8,128)(2,1)S(1)}, bf16[192,1024]{1,0:T(8,128)(2,1)S(1)}, u32[]{:S(2)}, u32[]{:S(2)}) collective-permute-start(bf16[192,1024]{1,0:T(8,128)(2,1)S(1)} %copy-done.28), channel_id=1, source_target_pairs={{0,28},{4,0},{8,4},{12,8},{16,12},{20,16},{24,20},{28,24},{1,29},{... | collective-permute-start | bytes 1179656 | tf_op jit(solution)/shard_map/ppermute | solution.py:21
  231.9 34.7 %collective-permute-start.19 = (bf16[192,1024]{1,0:T(8,128)(2,1)S(1)}, bf16[192,1024]{1,0:T(8,128)(2,1)S(1)}, u32[]{:S(2)}, u32[]{:S(2)}) collective-permute-start(bf16[192,1024]{1,0:T(8,128)(2,1)S(1)} %copy-done.27), channel_id=1, source_target_pairs={{0,28},{4,0},{8,4},{12,8},{16,12},{20,16},{24,20},{28,24},{1,29},{... | collective-permute-start | bytes 1179656 | tf_op jit(solution)/shard_map/ppermute | solution.py:21
  241.4 31.8 %collective-permute-start.9 = (bf16[192,1024]{1,0:T(8,128)(2,1)S(1)}, bf16[192,1024]{1,0:T(8,128)(2,1)S(1)}, u32[]{:S(2)}, u32[]{:S(2)}) collective-permute-start(bf16[192,1024]{1,0:T(8,128)(2,1)S(1)} %collective-permute-done.8), channel_id=1, source_target_pairs={{0,4},{4,8},{8,12},{12,16},{16,20},{20,24},{24,28},{28,0},{1,5},{5... | collective-permute-start | bytes 1179656 | tf_op jit(solution)/shard_map/ppermute | solution.py:19
  258.2 24.0 %collective-permute-start.17 = (bf16[192,1024]{1,0:T(8,128)(2,1)S(1)}, bf16[192,1024]{1,0:T(8,128)(2,1)S(1)}, u32[]{:S(2)}, u32[]{:S(2)}) collective-permute-start(bf16[192,1024]{1,0:T(8,128)(2,1)S(1)} %collective-permute-done.16), channel_id=1, source_target_pairs={{0,4},{4,8},{8,12},{12,16},{16,20},{20,24},{24,28},{28,0},{1,5},{5... | collective-permute-start | bytes 1179656 | tf_op jit(solution)/shard_map/ppermute | solution.py:19
  258.3 24.1 %collective-permute-start.13 = (bf16[192,1024]{1,0:T(8,128)(2,1)S(1)}, bf16[192,1024]{1,0:T(8,128)(2,1)S(1)}, u32[]{:S(2)}, u32[]{:S(2)}) collective-permute-start(bf16[192,1024]{1,0:T(8,128)(2,1)S(1)} %collective-permute-done.12), channel_id=1, source_target_pairs={{0,28},{4,0},{8,4},{12,8},{16,12},{20,16},{24,20},{28,24},{1,29},{... | collective-permute-start | bytes 1179656 | tf_op jit(solution)/shard_map/ppermute | solution.py:21
  266.7 20.0 %collective-permute-start.20 = (bf16[192,1024]{1,0:T(8,128)(2,1)S(1)}, bf16[192,1024]{1,0:T(8,128)(2,1)S(1)}, u32[]{:S(2)}, u32[]{:S(2)}) collective-permute-start(bf16[192,1024]{1,0:T(8,128)(2,1)S(1)} %collective-permute-done.19), channel_id=1, source_target_pairs={{0,28},{4,0},{8,4},{12,8},{16,12},{20,16},{24,20},{28,24},{1,29},{... | collective-permute-start | bytes 1179656 | tf_op jit(solution)/shard_map/ppermute | solution.py:21
  273.2 17.5 %collective-permute-start.10 = (bf16[192,1024]{1,0:T(8,128)(2,1)S(1)}, bf16[192,1024]{1,0:T(8,128)(2,1)S(1)}, u32[]{:S(2)}, u32[]{:S(2)}) collective-permute-start(bf16[192,1024]{1,0:T(8,128)(2,1)S(1)} %collective-permute-done.9), channel_id=1, source_target_pairs={{0,4},{4,8},{8,12},{12,16},{16,20},{20,24},{24,28},{28,0},{1,5},{5... | collective-permute-start | bytes 1179656 | tf_op jit(solution)/shard_map/ppermute | solution.py:19
  282.2 16.9 %collective-permute-start.18 = (bf16[192,1024]{1,0:T(8,128)(2,1)S(1)}, bf16[192,1024]{1,0:T(8,128)(2,1)S(1)}, u32[]{:S(2)}, u32[]{:S(2)}) collective-permute-start(bf16[192,1024]{1,0:T(8,128)(2,1)S(1)} %collective-permute-done.17), channel_id=1, source_target_pairs={{0,4},{4,8},{8,12},{12,16},{16,20},{20,24},{24,28},{28,0},{1,5},{5... | collective-permute-start | bytes 1179656 | tf_op jit(solution)/shard_map/ppermute | solution.py:19
  282.4 30.7 %collective-permute-start.14 = (bf16[192,1024]{1,0:T(8,128)(2,1)S(1)}, bf16[192,1024]{1,0:T(8,128)(2,1)S(1)}, u32[]{:S(2)}, u32[]{:S(2)}) collective-permute-start(bf16[192,1024]{1,0:T(8,128)(2,1)S(1)} %collective-permute-done.13), channel_id=1, source_target_pairs={{0,28},{4,0},{8,4},{12,8},{16,12},{20,16},{24,20},{28,24},{1,29},{... | collective-permute-start | bytes 1179656 | tf_op jit(solution)/shard_map/ppermute | solution.py:21
  286.7 26.4 %collective-permute-start.21 = (bf16[192,1024]{1,0:T(8,128)(2,1)S(1)}, bf16[192,1024]{1,0:T(8,128)(2,1)S(1)}, u32[]{:S(2)}, u32[]{:S(2)}) collective-permute-start(bf16[192,1024]{1,0:T(8,128)(2,1)S(1)} %collective-permute-done.20), channel_id=1, source_target_pairs={{0,28},{4,0},{8,4},{12,8},{16,12},{20,16},{24,20},{28,24},{1,29},{... | collective-permute-start | bytes 1179656 | tf_op jit(solution)/shard_map/ppermute | solution.py:21
  290.6 16.9 %collective-permute-start.11 = (bf16[192,1024]{1,0:T(8,128)(2,1)S(1)}, bf16[192,1024]{1,0:T(8,128)(2,1)S(1)}, u32[]{:S(2)}, u32[]{:S(2)}) collective-permute-start(bf16[192,1024]{1,0:T(8,128)(2,1)S(1)} %collective-permute-done.10), channel_id=1, source_target_pairs={{0,4},{4,8},{8,12},{12,16},{16,20},{20,24},{24,28},{28,0},{1,5},{5... | collective-permute-start | bytes 1179656 | tf_op jit(solution)/shard_map/ppermute | solution.py:19
  396.1 44.2 %copy-start.1 = (bf16[256,1536]{1,0:T(8,128)(2,1)S(1)}, bf16[256,1536]{1,0:T(8,128)(2,1)}, u32[]{:S(2)}) copy-start(bf16[256,1536]{1,0:T(8,128)(2,1)} %reduce-scatter.13.cloned.1.call-done) | copy-start | bytes 2359300
  396.1 44.2 %copy-start.35 = (f32[256]{0:T(256)S(1)}, f32[256]{0:T(256)}, u32[]{:S(2)}) copy-start(f32[256]{0:T(256)} %copy-done.34) | copy-start | bytes 3076
  396.1 46.6 %copy-start.3 = (bf16[256,1536]{1,0:T(8,128)(2,1)S(1)}, bf16[256,1536]{1,0:T(8,128)(2,1)}, u32[]{:S(2)}) copy-start(bf16[256,1536]{1,0:T(8,128)(2,1)} %param.13) | copy-start | bytes 2359300
  396.1 46.6 %copy-start.38 = (f32[256]{0:T(256)S(1)}, f32[256]{0:T(256)}, u32[]{:S(2)}) copy-start(f32[256]{0:T(256)} %get-tuple-element.43) | copy-start | bytes 3076
  396.1 93.5 %all-gather.16.cloned.1.call-start = ((), (), s32[]{:S(2)}) async-start(), calls=%async_computation.16 | async-start | bytes 3932160 | tf_op jit(solution)/shard_map/all_gather | solution.py:140
  442.7 10.5 %copy-start.40 = (f32[256]{0:T(256)}, f32[256]{0:T(256)S(1)}, u32[]{:S(2)}) copy-start(f32[256]{0:T(256)S(1)} %broadcast_multiply_fusion.1) | copy-start | bytes 3076
  445.5 105.7 %reduce-scatter.29.cloned.1.call-start = ((), (), s32[]{:S(2)}) async-start(), calls=%async_computation.22 | async-start | bytes 3538944 | tf_op jit(solution)/shard_map/reduce_scatter | solution.py:128
  463.5 132.7 %reduce-scatter.25.cloned.1.call-start = ((), (), s32[]{:S(2)}) async-start(), calls=%async_computation.20 | async-start | bytes 3538944 | tf_op jit(solution)/shard_map/reduce_scatter | solution.py:135
  471.2 169.7 %reduce-scatter.27.cloned.1.call-start = ((), (), s32[]{:S(2)}) async-start(), calls=%async_computation.21 | async-start | bytes 3538944 | tf_op jit(solution)/shard_map/reduce_scatter | solution.py:135
  479.1 10.5 %copy-start.23 = (bf16[1024,2,2,96]{0,3,2,1:T(8,128)(2,1)S(1)}, bf16[1024,2,2,96]{0,3,2,1:T(8,128)(2,1)}, u32[]{:S(2)}) copy-start(bf16[1024,2,2,96]{0,3,2,1:T(8,128)(2,1)} %copy-done.22) | copy-start | bytes 2359300
  479.2 196.4 %reduce-scatter.23.cloned.1.call-start = ((), (), s32[]{:S(2)}) async-start(), calls=%async_computation.19 | async-start | bytes 1327104 | tf_op jit(solution)/shard_map/reduce_scatter | solution.py:128
  497.6 11.8 %slice-start = ((s8[8388608]{0:T(1024)(128)(4,1)}), s8[4194304]{0:T(1024)(128)(4,1)S(1)}, s32[]{:S(2)}) async-start(s8[8388608]{0:T(1024)(128)(4,1)} %bitcast.219), calls=%async_computation.26 | async-start | bytes 8388608
  517.4 195.3 %reduce-scatter.21.cloned.1.call-start = ((), (), s32[]{:S(2)}) async-start(), calls=%async_computation.18 | async-start | bytes 2654208 | tf_op jit(solution)/shard_map/reduce_scatter | solution.py:135
  537.6 223.7 %reduce-scatter.19.cloned.1.call-start = ((), (), s32[]{:S(2)}) async-start(), calls=%async_computation.17 | async-start | bytes 3932160 | tf_op jit(solution)/shard_map/reduce_scatter | solution.py:143
  543.5 264.7 %reduce-scatter.15.cloned.1.call-start = ((), (), s32[]{:S(2)}) async-start(), calls=%async_computation.13 | async-start | bytes 3932160 | tf_op jit(solution)/shard_map/reduce_scatter | solution.py:143
  551.2 357.5 %reduce-scatter.31.cloned.1.call-start = ((), (), s32[]{:S(2)}) async-start(), calls=%async_computation.25 | async-start | bytes 811008
  551.2 127.1 %collective-permute-start.24 = (bf16[512,384]{1,0:T(8,128)(2,1)}, bf16[512,384]{1,0:T(8,128)(2,1)S(1)}, u32[]{:S(2)}, u32[]{:S(2)}) collective-permute-start(bf16[512,384]{1,0:T(8,128)(2,1)} %bitcast.252), channel_id=1, source_target_pairs={{0,0},{4,1},{8,2},{12,3},{16,4},{20,5},{24,6},{28,7},{1,8},{5,9},{... | collective-permute-start | bytes 1179656 | tf_op jit(solution)/shard_map/ppermute | solution.py:129
  642.9 165.2 %copy-start.4 = (bf16[256,1536]{1,0:T(8,128)(2,1)S(1)}, bf16[256,1536]{1,0:T(8,128)(2,1)}, u32[]{:S(2)}) copy-start(bf16[256,1536]{1,0:T(8,128)(2,1)} %param.13) | copy-start | bytes 2359300
  642.9 165.2 %copy-start.5 = (bf16[256,1536]{1,0:T(8,128)(2,1)S(1)}, bf16[256,1536]{1,0:T(8,128)(2,1)}, u32[]{:S(2)}) copy-start(bf16[256,1536]{1,0:T(8,128)(2,1)} %reduce-scatter.17.cloned.1.call-done) | copy-start | bytes 2359300
  675.6 3.8 collective-permute-start.23
  679.3 128.8 %copy-start.36 = (f32[256]{0:T(256)S(1)}, f32[256]{0:T(256)}, u32[]{:S(2)}) copy-start(f32[256]{0:T(256)} %copy-done.34) | copy-start | bytes 3076
  679.3 128.8 %copy-start.37 = (f32[256]{0:T(256)S(1)}, f32[256]{0:T(256)}, u32[]{:S(2)}) copy-start(f32[256]{0:T(256)} %get-tuple-element.42) | copy-start | bytes 3076
  679.3 128.9 %copy-start.39 = (f32[256]{0:T(256)S(1)}, f32[256]{0:T(256)}, u32[]{:S(2)}) copy-start(f32[256]{0:T(256)} %get-tuple-element.43) | copy-start | bytes 3076
  679.3 128.9 %copy-start.41 = (f32[256]{0:T(256)S(1)}, f32[256]{0:T(256)}, u32[]{:S(2)}) copy-start(f32[256]{0:T(256)} %copy-done.40) | copy-start | bytes 3076
  679.3 128.9 %copy-start.48 = (f32[256]{0:T(256)S(1)}, f32[256]{0:T(256)}, u32[]{:S(2)}) copy-start(f32[256]{0:T(256)} %get-tuple-element.41) | copy-start | bytes 3076
  (36 other events, 128.4 us)
Sparse Core Ops, SparseCore 0:
  10.2 34.4 all-gather.17
  46.6 43.4 all-gather.9
  167.0 47.6 reduce-scatter.12
  216.8 56.2 all-gather.19
  274.8 46.3 all-gather.13
  323.5 43.9 all-gather.11
  396.3 43.9 reduce-scatter.16
  445.6 43.9 all-gather.15
  491.9 40.3 reduce-scatter.28
  534.4 61.7 reduce-scatter.24
  598.5 42.3 reduce-scatter.26
  643.7 31.8 reduce-scatter.22
  677.9 34.7 reduce-scatter.20
  715.6 45.7 reduce-scatter.18
  764.2 43.9 reduce-scatter.14
  813.1 95.4 reduce-scatter.30
